TPU v7x, 32 devices: a whole 2x2x4 slice. The times are simulated.
32 devices in a mesh: parts: 2 (over y), tmpl: 4 (over z), sta: 4 (over x, core).
Axes of the slice: x: 2, y: 2, z: 4, core: 2. Of those that a mesh axis runs over, the one named last changes fastest.
Arguments:
- data: float32 [64, 3, 1280], P(('parts', 'sta'), None, 'tmpl'), parts along dimension 0, as said below
- templates: bfloat16 [32, 3, 16, 256], P('sta', None, 'tmpl'), as said below
- starts: int32 [32, 3, 16], P('sta', None, 'tmpl'), may hold values from 0 to 512
Outputs:
- network: float32 [32, 512], P(('parts', 'tmpl'), 'sta'), parts along dimension 0
There are 2 independent parts, one for each index of `parts`. A program takes and returns all parts, laid end to end along the dimension named above; an argument that names none is the same for every part. Nothing has to cross between parts.
Inputs may be any that keep to these rules, and one draw needn't show every extreme that they name: `data`: finite samples. `templates`: finite samples.
All inputs are finite; a program needn't handle non-finite values.
Results may differ from a plain program's by a relative error of at most 0.0029.
Values sent between devices are 32-bit elements; how exact they have to be, the bound alone decides.
A program may use at most 64 MiB of HBM per device.

v0:
```python
import jax
import jax.numpy as jnp
from jax import lax
from jax.sharding import PartitionSpec as P

TLEN = 256
MAXSHIFT = 512
LAGS = 512
EPS = 1e-06


def window_energy(trace):
    extent = LAGS + MAXSHIFT
    squares = trace * trace
    running = jnp.concatenate([jnp.zeros_like(squares[:, :1]), jnp.cumsum(squares, axis=1)], axis=1)
    return running[:, TLEN : TLEN + extent] - running[:, :extent]


def take_window(row, offset):
    return lax.dynamic_slice_in_dim(row, offset, LAGS, 0)


def local_term(whole, templates, starts):
    extent = LAGS + MAXSHIFT
    stations, channels, samples = whole.shape
    per_group = templates.shape[2]
    groups = stations * channels
    lowered = whole.astype(jnp.bfloat16).reshape(1, groups, samples)
    kernel = templates.reshape(groups * per_group, 1, templates.shape[-1])
    raw = lax.conv_general_dilated(
        lowered,
        kernel,
        (1,),
        "VALID",
        dimension_numbers=("NCH", "OIH", "NCH"),
        feature_group_count=groups,
        preferred_element_type=jnp.float32,
    )[0]
    raw = raw[:, :extent]
    energy = window_energy(whole.reshape(groups, samples))
    energy_rows = jnp.repeat(energy, per_group, axis=0)
    tnorm = jnp.sum(jnp.square(templates.astype(jnp.float32)), axis=-1).reshape(-1)
    offsets = starts.reshape(-1)
    slicer = jax.vmap(take_window)
    aligned = slicer(raw, offsets)
    local = slicer(energy_rows, offsets)
    scale = TLEN * jnp.sqrt((tnorm[:, None] / TLEN + EPS) * (local / TLEN + EPS))
    return jnp.sum((aligned / scale).reshape(groups, per_group, LAGS), axis=0)


def shards(data, templates, starts):
    whole = lax.all_gather(data, "tmpl", axis=2, tiled=True)
    partial_value = local_term(whole, templates, starts)
    summed = lax.psum(partial_value, "sta")
    width = LAGS // lax.axis_size("sta")
    return lax.dynamic_slice_in_dim(summed, lax.axis_index("sta") * width, width, 1)


def solution(mesh):
    return jax.shard_map(
        shards,
        mesh=mesh,
        in_specs=(
            P(("parts", "sta"), None, "tmpl"),
            P("sta", None, "tmpl", None),
            P("sta", None, "tmpl"),
        ),
        out_specs=P(("parts", "tmpl"), "sta"),
        check_vma=False,
    )
```

profile of v0, /device:TPU:0, one launch (start us, length us, event | category | flops | bytes accessed | tf_op | source)
XLA Modules:
  0.0 490.5 jit_solution(16499657202032533554)
XLA Ops:
  1.0 47.9 %all_gather.3 = f32[8,3,1280]{0,1,2:T(4,128)S(1)} all-gather(f32[8,3,320]{0,1,2:T(4,128)S(1)} %copy.29), channel_id=1, replica_groups=mesh['parts'=2,'tmpl'=4,'sta'=4] {'tmpl'}, dimensions={2}, use_global_device_ids=true | all-gather | bytes 153600 | tf_op jit(solution)/shard_map/all_gather | solution.py:52
  49.9 6.8 %reduce-window.6 = f32[24,10,128]{2,1,0:T(8,128)S(1)} reduce-window(f32[24,10,128]{2,1,0:T(8,128)S(1)} %mul.25, f32[]{:T(128)} %constant.9.clone.1), window={size=1x1x128 pad=0_0x0_0x127_0}, to_apply=%region_1.2 | reduce-window | flops 3901440 | bytes 245764 | tf_op jit(solution)/shard_map/reduce-window
  58.0 197.6 %while.3 = (s32[]{:T(128)}, f32[96,1024]{1,0:T(8,128)S(1)}, s32[96,2]{0,1:T(2,128)S(1)}, f32[96,512]{1,0:T(8,128)S(1)}, s32[]{:T(128)}, /*index=5*/s32[]{:T(128)}) while((s32[]{:T(128)}, f32[96,1024]{1,0:T(8,128)S(1)}, s32[96,2]{0,1:T(2,128)S(1)}, f32[96,512]{1,0:T(8,128)S(1)}, s32[]{:T(128)}, /*index=5*/s32[]{:T(128)}) %tuple.38), condition=%wide.while_cond.1, body=%wide.while_body.1.sunk | while | flops 2 | bytes 8305 | solution.py:20
  75.2 1.3 dynamic-slice.15
  77.2 1.3 dynamic-slice.15
  79.3 1.3 dynamic-slice.15
  81.3 1.3 dynamic-slice.15
  83.4 1.3 dynamic-slice.15
  85.5 1.3 dynamic-slice.15
  87.5 1.3 dynamic-slice.15
  89.6 1.3 dynamic-slice.15
  91.6 1.3 dynamic-slice.15
  114.3 1.3 dynamic-slice.15
  116.3 1.3 dynamic-slice.15
  118.4 1.3 dynamic-slice.15
  120.5 1.3 dynamic-slice.15
  122.5 1.3 dynamic-slice.15
  124.6 1.3 dynamic-slice.15
  126.6 1.3 dynamic-slice.15
  128.7 1.3 dynamic-slice.15
  130.7 1.3 dynamic-slice.15
  256.5 28.5 %fusion.1 = f32[1,96,1025]{1,0,2:T(1,128)S(1)} fusion(bf16[1,24,1280]{1,0,2:T(2,128)(2,1)S(1)} %copy.33, s32[96]{0:T(128)S(1)} %copy-done.2, bf16[96,256]{0,1:T(8,128)(2,1)S(1)} %copy.32), kind=kOutput, calls=%fused_computation.4 | convolution fusion | flops 1210318848 | bytes 504576 | tf_op jit(solution)/shard_map/conv_general_dilated | solution.py:30
  285.8 197.6 %while.2 = (s32[]{:T(128)}, f32[96,1024]{1,0:T(8,128)S(1)}, s32[96,2]{0,1:T(2,128)S(1)}, f32[96,512]{1,0:T(8,128)S(1)}, s32[]{:T(128)}, /*index=5*/s32[]{:T(128)}) while((s32[]{:T(128)}, f32[96,1024]{1,0:T(8,128)S(1)}, s32[96,2]{0,1:T(2,128)S(1)}, f32[96,512]{1,0:T(8,128)S(1)}, s32[]{:T(128)}, /*index=5*/s32[]{:T(128)}) %tuple.41), condition=%wide.while_cond, body=%wide.while_body.sunk | while | flops 2 | bytes 8305 | solution.py:20
  484.1 5.8 %psum.7 = f32[4,512]{1,0:T(4,128)S(1)} all-reduce(f32[4,512]{1,0:T(4,128)S(1)} %fusion.5), channel_id=1, replica_groups=mesh['parts'=2,'tmpl'=4,'sta'=4] {'sta'}, use_global_device_ids=true, to_apply=%region_4.5 | all-reduce | flops 2048 | bytes 16384 | tf_op jit(solution)/shard_map/psum | solution.py:54
  (794 shorter events, 372.8 us)
Async XLA Ops:
  56.7 1.0 copy-start.1
  57.6 198.7 %copy-start = (bf16[8,3,4,256]{3,2,1,0:T(4,128)(2,1)S(1)}, bf16[8,3,4,256]{3,2,1,0:T(4,128)(2,1)}, u32[]{:S(2)}) copy-start(bf16[8,3,4,256]{3,2,1,0:T(4,128)(2,1)} %param.4) | copy-start | bytes 147460
  57.6 198.9 %copy-start.2 = (s32[96]{0:T(128)S(1)}, s32[96]{0:T(128)}, u32[]{:S(2)}) copy-start(s32[96]{0:T(128)} %constant.11.clone.1) | copy-start | bytes 1156
where the time goes:
time: 494 us; the launch traced here: 490 us
  local copies, waits for them, and re-layouts  396 us (80%)
  blocking collectives  53.7 us (11%)
  matrix products  28.5 us (6%)
  other arithmetic  7.52 us (2%)
    gather x768, local copies, waits for them, and re-layouts  391 us
    all_gather x1, blocking collectives, shards(): whole = lax.all_gather(data, 'tmpl', axis=2, tiled=True)  47.9 us
    conv_general_dilated x1, matrix products, local_term(): lax.conv_general_dilated(lowered, kernel, (1,), 'VALID', dimension_number...  28.5 us

commit v1 on v0

--- a/solution.py
+++ b/solution.py
@@ -7,6 +7,17 @@
 MAXSHIFT = 512
 LAGS = 512
 EPS = 1e-06
+
+
+def gather_around(x, axis, dim):
+    ways = lax.axis_size(axis)
+    pieces = [x]
+    for far in range(1, ways):
+        pieces.append(
+            lax.ppermute(pieces[far - 1], axis, [(d, (d - 1) % ways) for d in range(ways)])
+        )
+    line = jnp.concatenate(pieces, axis=dim)
+    return jnp.roll(line, lax.axis_index(axis) * x.shape[dim], axis=dim)
 
 
 def window_energy(trace):
@@ -49,7 +60,7 @@
 
 
 def shards(data, templates, starts):
-    whole = lax.all_gather(data, "tmpl", axis=2, tiled=True)
+    whole = gather_around(data, "tmpl", 2)
     partial_value = local_term(whole, templates, starts)
     summed = lax.psum(partial_value, "sta")
     width = LAGS // lax.axis_size("sta")

time: 494 us -> 463 us (0.937)
  blocking collectives: 53.7 us -> 5.77 us
  starting transfers between devices: 0 us -> 13.2 us
    all_gather x1 -> x0, blocking collectives: 47.9 us -> none  [shards(): whole = lax.all_gather(data, 'tmpl', axis=2, tiled=True)]
    ppermute x0 -> x3, starting transfers between devices: none -> 13.2 us  [gather_around(): lax.ppermute(pieces[far - 1], axis, [(d, (d - 1) % ways) for d in range(w...]
  transfers between devices with their start and end apart: 0 -> 3, of which waited for: 0 -> 2; matrix products, arithmetic and copies ran while one was open for 0% -> 1% of each run, Pallas kernels for 0% -> 0%
where the time goes in v1:
time: 463 us; the launch traced here: 460 us
  local copies, waits for them, and re-layouts  397 us (86%)
  matrix products  28.5 us (6%)
  starting transfers between devices  13.2 us (3%)
  other arithmetic  8.38 us (2%)
  blocking collectives  5.77 us (1%)
  loops' own time  4.65 us (1%)
    gather x768, local copies, waits for them, and re-layouts  391 us
    conv_general_dilated x1, matrix products, local_term(): lax.conv_general_dilated(lowered, kernel, (1,), 'VALID', dimension_number...  28.5 us
    ppermute x3, starting transfers between devices, gather_around(): lax.ppermute(pieces[far - 1], axis, [(d, (d - 1) % ways) for d in range(w...  13.2 us
  transfers between devices with their start and end apart: 3, of which 2 were waited for; matrix products, arithmetic and copies ran while one was open for 1% of the time, Pallas kernels for 0%

profile of v1, /device:TPU:0, one launch (start us, length us, event | category | flops | bytes accessed | tf_op | source)
XLA Modules:
  0.0 459.5 jit_solution(16802766882999763056)
XLA Ops:
  0.0 5.0 %collective-permute-start = (f32[8,3,320]{2,0,1:T(8,128)}, f32[8,3,320]{2,0,1:T(8,128)S(1)}, u32[]{:S(2)}, u32[]{:S(2)}) collective-permute-start(f32[8,3,320]{2,0,1:T(8,128)} %param.3), channel_id=1, source_target_pairs={{0,12},{4,0},{8,4},{12,8},{1,13},{5,1},{9,5},{13,9},{2,14},{6,2},{... | collective-permute-start | bytes 92168 | tf_op jit(solution)/shard_map/ppermute | solution.py:17
  7.0 4.0 collective-permute-start.1
  11.0 1.6 collective-permute-done.1
  12.7 4.1 collective-permute-start.2
  19.8 6.8 %reduce-window.6 = f32[24,10,128]{2,1,0:T(8,128)S(1)} reduce-window(f32[24,10,128]{2,1,0:T(8,128)S(1)} %mul.29, f32[]{:T(128)} %constant.50.clone.1), window={size=1x1x128 pad=0_0x0_0x127_0}, to_apply=%region_1.2 | reduce-window | flops 3901440 | bytes 245764 | tf_op jit(solution)/shard_map/reduce-window
  27.6 197.6 %while.3 = (s32[]{:T(128)}, f32[96,1024]{1,0:T(8,128)S(1)}, s32[96,2]{0,1:T(2,128)S(1)}, f32[96,512]{1,0:T(8,128)S(1)}, s32[]{:T(128)}, /*index=5*/s32[]{:T(128)}) while((s32[]{:T(128)}, f32[96,1024]{1,0:T(8,128)S(1)}, s32[96,2]{0,1:T(2,128)S(1)}, f32[96,512]{1,0:T(8,128)S(1)}, s32[]{:T(128)}, /*index=5*/s32[]{:T(128)}) %tuple.37), condition=%wide.while_cond.1, body=%wide.while_body.1.sunk | while | flops 2 | bytes 8305 | solution.py:31
  48.8 1.3 dynamic-slice.15
  50.9 1.3 dynamic-slice.15
  52.9 1.3 dynamic-slice.15
  55.0 1.3 dynamic-slice.15
  57.1 1.3 dynamic-slice.15
  59.1 1.3 dynamic-slice.15
  61.2 1.3 dynamic-slice.15
  63.2 1.3 dynamic-slice.15
  65.3 1.3 dynamic-slice.15
  87.9 1.3 dynamic-slice.15
  90.0 1.3 dynamic-slice.15
  92.1 1.3 dynamic-slice.15
  94.1 1.3 dynamic-slice.15
  96.2 1.3 dynamic-slice.15
  98.2 1.3 dynamic-slice.15
  225.9 28.5 %fusion.1 = f32[1,96,1025]{1,0,2:T(1,128)S(1)} fusion(bf16[1,24,1280]{1,0,2:T(2,128)(2,1)S(1)} %copy.30, s32[96]{0:T(128)S(1)} %copy-done, bf16[96,256]{0,1:T(8,128)(2,1)S(1)} %copy.29), kind=kOutput, calls=%fused_computation.4 | convolution fusion | flops 1210318848 | bytes 504576 | tf_op jit(solution)/shard_map/conv_general_dilated | solution.py:41
  255.2 197.6 %while.2 = (s32[]{:T(128)}, f32[96,1024]{1,0:T(8,128)S(1)}, s32[96,2]{0,1:T(2,128)S(1)}, f32[96,512]{1,0:T(8,128)S(1)}, s32[]{:T(128)}, /*index=5*/s32[]{:T(128)}) while((s32[]{:T(128)}, f32[96,1024]{1,0:T(8,128)S(1)}, s32[96,2]{0,1:T(2,128)S(1)}, f32[96,512]{1,0:T(8,128)S(1)}, s32[]{:T(128)}, /*index=5*/s32[]{:T(128)}) %tuple.40), condition=%wide.while_cond, body=%wide.while_body.sunk | while | flops 2 | bytes 8305 | solution.py:31
  453.2 5.8 %psum.7 = f32[4,512]{1,0:T(4,128)S(1)} all-reduce(f32[4,512]{1,0:T(4,128)S(1)} %fusion.5), channel_id=1, replica_groups=mesh['parts'=2,'tmpl'=4,'sta'=4] {'sta'}, use_global_device_ids=true, to_apply=%region_4.5 | all-reduce | flops 2048 | bytes 16384 | tf_op jit(solution)/shard_map/psum | solution.py:65
  (795 shorter events, 378.9 us)
Async XLA Ops:
  0.0 7.0 %collective-permute-start = (f32[8,3,320]{2,0,1:T(8,128)}, f32[8,3,320]{2,0,1:T(8,128)S(1)}, u32[]{:S(2)}, u32[]{:S(2)}) collective-permute-start(f32[8,3,320]{2,0,1:T(8,128)} %param.3), channel_id=1, source_target_pairs={{0,12},{4,0},{8,4},{12,8},{1,13},{5,1},{9,5},{13,9},{2,14},{6,2},{... | collective-permute-start | bytes 92168 | tf_op jit(solution)/shard_map/ppermute | solution.py:17
  7.0 5.7 %collective-permute-start.1 = (f32[8,3,320]{2,0,1:T(8,128)S(1)}, f32[8,3,320]{2,0,1:T(8,128)S(1)}, u32[]{:S(2)}, u32[]{:S(2)}) collective-permute-start(f32[8,3,320]{2,0,1:T(8,128)S(1)} %collective-permute-done), channel_id=1, source_target_pairs={{0,12},{4,0},{8,4},{12,8},{1,13},{5,1},{9,5},{13,9},{2,14},{6,2},{... | collective-permute-start | bytes 92168 | tf_op jit(solution)/shard_map/ppermute | solution.py:17
  12.7 5.8 %collective-permute-start.2 = (f32[8,3,320]{2,0,1:T(8,128)S(1)}, f32[8,3,320]{2,0,1:T(8,128)S(1)}, u32[]{:S(2)}, u32[]{:S(2)}) collective-permute-start(f32[8,3,320]{2,0,1:T(8,128)S(1)} %collective-permute-done.1), channel_id=1, source_target_pairs={{0,12},{4,0},{8,4},{12,8},{1,13},{5,1},{9,5},{13,9},{2,14},{6,2},{... | collective-permute-start | bytes 92168 | tf_op jit(solution)/shard_map/ppermute | solution.py:17
  225.2 0.7 copy-start
